TPU v7x, 32 devices: a whole 2x2x4 slice. The times are simulated.
32 devices in a mesh: grp: 2 (over x), seq: 4 (over y, core), sub: 4 (over z).
Axes of the slice: x: 2, y: 2, z: 4, core: 2. Of those that a mesh axis runs over, the one named last changes fastest.
Arguments:
- query_rows: bfloat16 [8, 512, 2048], P(('grp', 'sub'), 'seq'), parts along dimension 0, may hold values from -9 to 9
- key_rows: bfloat16 [8, 512, 256], P(('grp', 'sub'), 'seq'), parts along dimension 0, may hold values from -4 to 4
- value_rows: bfloat16 [8, 512, 256], P(('grp', 'sub'), 'seq'), parts along dimension 0, may hold values from -6 to 6
- residual_in: bfloat16 [8, 512, 2048], P(('grp', 'sub'), 'seq'), parts along dimension 0, may hold values from -6 to 6
- out_proj: bfloat16 [2048, 2048], P('seq'), may hold values from -0.5 to 0.5
- norm_gain: bfloat16 [2048], replicated, may hold values from 0.099609375 to 1.8984375
- expert_ids: int32 [8, 512, 8], P(('grp', 'sub'), 'seq'), parts along dimension 0, may hold values from 0 to 15, all different within a row; in each aligned block of 128 rows (0 to 127, 128 to 255, ..., all dimensions but the last counted through in order) at most 80 rows name the same one
- gate_weights: bfloat16 [8, 512, 8], P(('grp', 'sub'), 'seq'), parts along dimension 0, may hold values from 0.049804688 to 1
- expert_gate: bfloat16 [16, 2048, 768], P(('seq', 'sub')), may hold values from -0.125 to 0.125
- expert_up: bfloat16 [16, 2048, 768], P(('seq', 'sub')), may hold values from -0.125 to 0.125
- expert_down: bfloat16 [16, 768, 2048], P(('seq', 'sub')), may hold values from -0.21875 to 0.21875
Outputs:
- layer_out: bfloat16 [8, 512, 2048], P(('grp', 'sub'), 'seq'), parts along dimension 0
There are 2 independent parts, one for each index of `grp`. A program takes and returns all parts, laid end to end along the dimension named above; an argument that names none is the same for every part. Nothing has to cross between parts.
Inputs may be any that keep to these rules, and one draw needn't show every extreme that they name: `expert_ids`: A row names 8 different experts. In each aligned block of 128 rows (the rows of one device) no expert is named by more than 80 rows, a bound that some block reaches.
All inputs are finite; a program needn't handle non-finite values.
Results may differ from a plain program's by a relative error of at most 0.013.
Values may be sent and summed in bfloat16 or wider, within the bound.
A program may use at most 128 MiB of HBM per device.

v0:
```python
import jax
import jax.numpy as jnp
from jax import lax
from jax.sharding import PartitionSpec as P

D = 2048
HD = 128
QH = 16
KVH = 2


def attend_head(queries, keys_one, values_one, block):
    length = queries.shape[0]
    scale = 1.0 / queries.shape[1] ** 0.5
    pieces = []
    for part_index in range(length // block):
        stop = (part_index + 1) * block
        rows_here = queries[part_index * block : stop]
        scores = (
            jnp.einsum("qd,kd->qk", rows_here, keys_one[:stop], preferred_element_type=jnp.float32)
            * scale
        )
        row_pos = part_index * block + jnp.arange(block, dtype=jnp.int32)
        col_pos = jnp.arange(stop, dtype=jnp.int32)
        scores = jnp.where(row_pos[:, None] >= col_pos[None, :], scores, -1e30)
        peak = jnp.max(scores, axis=1, keepdims=True)
        weights = jnp.exp(scores - peak)
        probs = (weights / jnp.sum(weights, axis=1, keepdims=True)).astype(jnp.bfloat16)
        pieces.append(
            jnp.dot(probs, values_one[:stop], preferred_element_type=jnp.float32).astype(
                jnp.bfloat16
            )
        )
    return jnp.concatenate(pieces, axis=0)


def rank_in_expert(flat_ids, experts):
    items = flat_ids.shape[0]
    width = 128
    n_parts = items // width
    onehot = (
        (flat_ids[:, None] == jnp.arange(experts, dtype=jnp.int32)[None, :])
        .astype(jnp.bfloat16)
        .reshape(n_parts, width, experts)
    )
    lower = (
        jnp.arange(width, dtype=jnp.int32)[:, None] > jnp.arange(width, dtype=jnp.int32)[None, :]
    ).astype(jnp.bfloat16)
    within = jnp.einsum("ij,bje->bie", lower, onehot, preferred_element_type=jnp.float32)
    part_counts = jnp.sum(onehot.astype(jnp.float32), axis=1)
    earlier = jnp.cumsum(part_counts, axis=0) - part_counts
    ranks = jnp.sum((within + earlier[:, None, :]) * onehot.astype(jnp.float32), axis=2)
    return ranks.reshape(items).astype(jnp.int32)


def per_device(
    query_rows,
    key_rows,
    value_rows,
    residual_in,
    out_proj,
    norm_gain,
    expert_ids,
    gate_weights,
    expert_gate,
    expert_up,
    expert_down,
):
    tokens = query_rows.shape[1]
    n_seq = lax.axis_size("seq")
    n_sub = lax.axis_size("sub")
    heads_here = QH // n_seq
    group = QH // KVH
    query_local = lax.all_to_all(query_rows, "seq", split_axis=2, concat_axis=1, tiled=True)
    key_full, value_full = (
        lax.all_gather(key_rows, "seq", axis=1, tiled=True),
        lax.all_gather(value_rows, "seq", axis=1, tiled=True),
    )
    first_head = lax.axis_index("seq") * heads_here
    key_list = []
    value_list = []
    for head in range(heads_here):
        kv_start = (first_head + head) // group * HD
        key_list.append(lax.dynamic_slice_in_dim(key_full[0], kv_start, HD, 1))
        value_list.append(lax.dynamic_slice_in_dim(value_full[0], kv_start, HD, 1))
    length = query_local.shape[1]
    block = min(length, max(512, length // 8))
    outputs = [
        attend_head(
            query_local[0, :, head * HD : (head + 1) * HD], key_list[head], value_list[head], block
        )
        for head in range(heads_here)
    ]
    head_block = jnp.concatenate(outputs, axis=1)[None]
    attended = lax.all_to_all(head_block, "seq", split_axis=1, concat_axis=2, tiled=True)[0]
    projected = jnp.dot(
        attended,
        lax.all_gather(out_proj, "seq", axis=0, tiled=True),
        preferred_element_type=jnp.float32,
    )
    hidden = (residual_in[0].astype(jnp.float32) + projected).astype(jnp.bfloat16)
    wide = hidden.astype(jnp.float32)
    normed = (
        wide
        * lax.rsqrt(jnp.mean(wide * wide, axis=1, keepdims=True) + 1e-06)
        * norm_gain.astype(jnp.float32)
    ).astype(jnp.bfloat16)
    topk = expert_ids.shape[2]
    experts = n_seq * n_sub
    cap = max(2, (5 * tokens * topk + 4 * experts - 1) // (4 * experts))
    flat_ids = expert_ids[0].reshape(-1)
    items = flat_ids.shape[0]
    ranks = rank_in_expert(flat_ids, experts)
    slot_of = flat_ids * cap + ranks
    slots_out = experts * cap
    item_of_slot = (
        jnp.full((slots_out,), items, jnp.int32).at[slot_of].set(jnp.arange(items, dtype=jnp.int32))
    )
    padded_rows = jnp.concatenate([normed, jnp.zeros((1, D), jnp.bfloat16)], axis=0)
    padded_gates = jnp.concatenate(
        [gate_weights[0].reshape(-1), jnp.zeros((1,), jnp.bfloat16)], axis=0
    )
    token_of_slot = jnp.where(item_of_slot < items, item_of_slot // topk, tokens)
    send_rows = padded_rows[token_of_slot].reshape(experts, cap, D)
    send_gates = padded_gates[item_of_slot].reshape(experts, cap)
    recv_rows, recv_gates = (
        lax.all_to_all(send_rows, ("seq", "sub"), split_axis=0, concat_axis=0, tiled=True),
        lax.all_to_all(send_gates, ("seq", "sub"), split_axis=0, concat_axis=0, tiled=True),
    )
    slots_in = experts * cap
    valid = recv_gates > 0
    counts = jnp.sum(valid.astype(jnp.int32), axis=1)
    offsets = jnp.cumsum(counts) - counts
    dest = jnp.where(
        valid, offsets[:, None] + jnp.arange(cap, dtype=jnp.int32)[None, :], slots_in
    ).reshape(-1)
    source_of = (
        jnp.full((slots_in + 1,), slots_in, jnp.int32)
        .at[dest]
        .set(jnp.arange(slots_in, dtype=jnp.int32))[:slots_in]
    )
    compact_rows = jnp.concatenate(
        [recv_rows.reshape(slots_in, D), jnp.zeros((1, D), jnp.bfloat16)], axis=0
    )[source_of]
    compact_gates = jnp.concatenate(
        [recv_gates.reshape(-1), jnp.zeros((1,), jnp.bfloat16)], axis=0
    )[source_of].astype(jnp.float32)
    filled = jnp.sum(counts)
    n_blocks = (filled + slots_in - 1) // slots_in
    w_gate = expert_gate[0]
    w_up = expert_up[0]
    w_down = expert_down[0]

    def expert_block(index, results):
        gate_proj = jnp.dot(compact_rows, w_gate, preferred_element_type=jnp.float32)
        up_proj = jnp.dot(compact_rows, w_up, preferred_element_type=jnp.float32)
        inner = (jax.nn.silu(gate_proj) * up_proj).astype(jnp.bfloat16)
        weighted = (
            jnp.dot(inner, w_down, preferred_element_type=jnp.float32) * compact_gates[:, None]
        )
        return weighted.astype(jnp.bfloat16)

    results = lax.fori_loop(0, n_blocks, expert_block, jnp.zeros((slots_in, D), jnp.bfloat16))
    returned = jnp.concatenate([results, jnp.zeros((1, D), jnp.bfloat16)], axis=0)[dest].reshape(
        experts, cap, D
    )
    back = lax.all_to_all(
        returned, ("seq", "sub"), split_axis=0, concat_axis=0, tiled=True
    ).reshape(slots_out, D)
    gathered = back[slot_of].reshape(tokens, topk, D).astype(jnp.float32)
    mixture = jnp.sum(gathered, axis=1)
    return (wide + mixture).astype(jnp.bfloat16)[None]


def solution(mesh):
    placed = (
        P(("grp", "sub"), "seq", None),
        P(("grp", "sub"), "seq", None),
        P(("grp", "sub"), "seq", None),
        P(("grp", "sub"), "seq", None),
        P("seq", None),
        P(),
        P(("grp", "sub"), "seq", None),
        P(("grp", "sub"), "seq", None),
        P(("seq", "sub"), None, None),
        P(("seq", "sub"), None, None),
        P(("seq", "sub"), None, None),
    )
    return jax.shard_map(
        per_device,
        mesh=mesh,
        in_specs=placed,
        out_specs=P(("grp", "sub"), "seq", None),
        check_vma=False,
    )
```

profile of v0, /device:TPU:0, one launch (start us, length us, event | category | flops | bytes accessed | tf_op | source)
XLA Modules:
  0.0 475.6 jit_solution(11727438130950992658)
XLA Ops:
  7.3 3.7 copy.33
  11.6 13.3 %reduce.9 = bf16[2048,128]{1,0:T(8,128)(2,1)} reduce(bf16[2048,1,128]{2,1,0:T(2,128)(2,1)} %bitcast.127, bf16[]{:T(256)} %broadcast.193), dimensions={1}, to_apply=%bitcast.95.reduce_sub_computation | reduce | bytes 1048578
  26.9 4.3 all-to-all-start
  32.2 18.7 %all_gather.9 = bf16[1,512,256]{2,1,0:T(8,128)(2,1)} all-gather(bf16[1,128,256]{2,1,0:T(8,128)(2,1)S(1)} %copy-done.6), channel_id=1, replica_groups=mesh['grp'=2,'seq'=4,'sub'=4] {'seq'}, dimensions={1}, use_global_device_ids=true | all-gather | bytes 327680 | tf_op jit(solution)/shard_map/all_gather | solution.py:76
  50.9 8.0 %all_gather.10 = bf16[1,512,256]{2,1,0:T(8,128)(2,1)S(1)} all-gather(bf16[1,128,256]{2,1,0:T(8,128)(2,1)S(1)} %copy-done.7), channel_id=1, replica_groups=mesh['grp'=2,'seq'=4,'sub'=4] {'seq'}, dimensions={1}, use_global_device_ids=true | all-gather | bytes 327680 | tf_op jit(solution)/shard_map/all_gather | solution.py:77
  58.9 3.5 reshape.277
  74.7 3.6 copy.35
  78.3 5.5 %reduce.10 = bf16[512,512]{1,0:T(8,128)(2,1)} reduce(bf16[512,1,512]{2,1,0:T(2,128)(2,1)} %bitcast.126, bf16[]{:T(256)} %broadcast.193), dimensions={1}, to_apply=%bitcast.97.reduce_sub_computation | reduce | bytes 1048578
  86.1 4.1 all-to-all-start.1
  90.3 4.3 scatter_custom_fusion
  94.7 8.0 %gather_fusion = bf16[1280]{0:T(1024)(128)(2,1)S(1)} fusion(bf16[1025]{0:T(1024)(128)(2,1)S(1)} %pad_maximum_fusion, s32[2048]{0:T(1024)S(1)} %get-tuple-element.173), kind=kCustom, calls=%fused_computation | custom fusion | bytes 10240 | tf_op jit(solution)/shard_map/gather | solution.py:125
  103.4 7.5 %all-to-all-start.2 = ((bf16[16,1,80]{2,1,0:T(2,128)(2,1)}), bf16[16,1,80]{2,1,0:T(2,128)(2,1)S(1)}, u32[]{:S(2)}, u32[]{:S(2)}) async-start(bf16[16,1,80]{2,1,0:T(2,128)(2,1)} %all_to_all.47), calls=%async_computation.2 | async-start | bytes 16384 | tf_op jit(solution)/shard_map/all_to_all | solution.py:128
  110.9 3.5 reshape.279
  118.6 4.9 %multiply_reduce_fusion = (f32[128]{0:T(128)S(1)}, f32[128,2048]{1,0:T(8,128)S(1)}) fusion(bf16[128,2048]{0,1:T(8,128)(2,1)} %bitcast.128, bf16[2048,2048]{1,0:T(8,128)(2,1)} %all-gather.2.cloned.1.call-done, bf16[1,128,2048]{2,1,0:T(8,128)(2,1)} %param.16), kind=kOutput, calls=%fused_computation.42 | convolution fusion | flops 1075314560 | bytes 10486272 | tf_op jit(solution)/shard_map/dot_general | solution.py:96
  125.6 11.9 %gather_fusion.2 = bf16[1280,2048]{1,0:T(8,128)(2,1)} fusion(bf16[129,2048]{1,0:T(8,128)(2,1)} %concatenate.21, s32[2048]{0:T(1024)S(1)} %get-tuple-element.172), kind=kCustom, calls=%fused_computation.2 | custom fusion | bytes 10490880 | tf_op jit(solution)/shard_map/gather | solution.py:124
  137.5 6.1 %all-to-all-start.3 = ((bf16[16,80,2048]{2,1,0:T(8,128)(2,1)}), bf16[16,80,2048]{2,1,0:T(8,128)(2,1)}, u32[]{:S(2)}, u32[]{:S(2)}) async-start(bf16[16,80,2048]{2,1,0:T(8,128)(2,1)} %bitcast.122), calls=%async_computation.3 | async-start | bytes 10485760 | tf_op jit(solution)/shard_map/all_to_all | solution.py:127
  146.0 5.4 %scatter_custom_fusion.1 = s32[1281]{0:T(1024)S(1)} fusion(s32[1280]{0:T(1024)S(1)} %fusion.47, s32[1280]{0:T(1024)S(1)} %iota.44, s32[]{:T(128)} %constant.125.clone.1), kind=kCustom, calls=%fused_computation.109 | custom fusion | bytes 5128 | tf_op jit(solution)/shard_map/scatter | solution.py:140
  151.5 8.0 %gather_fusion.1 = bf16[1280]{0:T(1024)(128)(2,1)S(1)} fusion(bf16[1281]{0:T(1024)(128)(2,1)S(1)} %pad_maximum_fusion.1, s32[2048]{0:T(1024)S(1)} %pad_clamp_fusion.2), kind=kCustom, calls=%fused_computation.1 | custom fusion | bytes 10240 | tf_op jit(solution)/shard_map/gather | solution.py:145
  159.5 101.0 %all-to-all-done.3 = bf16[16,80,2048]{2,1,0:T(8,128)(2,1)} async-done(((bf16[16,80,2048]{2,1,0:T(8,128)(2,1)}), bf16[16,80,2048]{2,1,0:T(8,128)(2,1)}, u32[]{:S(2)}, u32[]{:S(2)}) %all-to-all-start.3) | async-done | bytes 5242912 | tf_op jit(solution)/shard_map/all_to_all | solution.py:127
  260.5 5.7 %concatenate.22 = bf16[1281,2048]{1,0:T(8,128)(2,1)} pad(bf16[1280,2048]{1,0:T(8,128)(2,1)} %bitcast.28, bf16[]{:T(256)} %constant.121.clone.1), padding=0_1x0_0 | pad | bytes 10489858 | tf_op jit(solution)/shard_map/concatenate | solution.py:142
  266.1 14.0 %gather_fusion.3 = bf16[1280,2048]{1,0:T(8,128)(2,1)} fusion(bf16[1281,2048]{1,0:T(8,128)(2,1)} %concatenate.22, s32[2048]{0:T(1024)S(1)} %pad_clamp_fusion.2), kind=kCustom, calls=%fused_computation.3 | custom fusion | bytes 10490880 | tf_op jit(solution)/shard_map/gather | solution.py:142
  280.1 7.2 %fusion.4 = f32[1280,768]{1,0:T(8,128)S(1)} fusion(bf16[1280,2048]{1,0:T(8,128)(2,1)} %gather_fusion.3, bf16[1,2048,768]{2,1,0:T(8,128)(2,1)} %param.21), kind=kOutput, calls=%fused_computation.15 | convolution fusion | flops 4026531840 | bytes 12320768 | tf_op jit(solution)/shard_map/while/body/dot_general | solution.py:155
  287.4 4.8 %fusion = bf16[1280,768]{1,0:T(8,128)(2,1)S(1)} fusion(bf16[1280,2048]{1,0:T(8,128)(2,1)S(1)} %copy-done.4, f32[1280,768]{1,0:T(8,128)S(1)} %fusion.4, bf16[1,2048,768]{2,1,0:T(8,128)(2,1)S(1)} %copy-done.11), kind=kOutput, calls=%fused_computation.11 | convolution fusion | flops 4032430080 | bytes 14286848 | tf_op jit(solution)/shard_map/while/body/dot_general | solution.py:156
  292.2 6.9 %fusion.1 = f32[1280,2048]{1,0:T(8,128)} fusion(bf16[1280,768]{1,0:T(8,128)(2,1)S(1)} %fusion, bf16[1,768,2048]{2,1,0:T(8,128)(2,1)S(1)} %copy-done), kind=kOutput, calls=%fused_computation.12 | convolution fusion | flops 4026531840 | bytes 15597568 | tf_op jit(solution)/shard_map/while/body/dot_general | solution.py:159
  302.1 7.1 %while.14 = (s32[]{:T(128)}, bf16[1280,2048]{1,0:T(8,128)(2,1)}, s32[]{:T(128)}, f32[1280]{0:T(1024)S(1)}, f32[1280,2048]{1,0:T(8,128)}, /*index=5*/s32[]{:T(128)}) while((s32[]{:T(128)}, bf16[1280,2048]{1,0:T(8,128)(2,1)}, s32[]{:T(128)}, f32[1280]{0:T(1024)S(1)}, f32[1280,2048]{1,0:T(8,128)}, /*index=5*/s32[]{:T(128)}) %tuple.40), condition=%wide.region_18.19_spmd, body=%wide.region_17.18_spmd.sunk | while | flops 5242882 | bytes 15733829 | solution.py:163
  302.1 7.0 %multiply_convert_fusion.3 = bf16[1280,2048]{1,0:T(8,128)(2,1)} fusion(f32[1280,2048]{1,0:T(8,128)} %get-tuple-element.220, f32[1280]{0:T(1024)S(1)} %get-tuple-element.219), kind=kLoop, calls=%fused_computation.8.clone.1 | loop fusion | flops 5242880 | bytes 15733760 | tf_op jit(solution)/shard_map/while/body/convert_element_type | solution.py:161
  309.3 5.7 %concatenate.23 = bf16[1281,2048]{1,0:T(8,128)(2,1)} pad(bf16[1280,2048]{1,0:T(8,128)(2,1)} %get-tuple-element.147, bf16[]{:T(256)} %constant.121.clone.1), padding=0_1x0_0 | pad | bytes 10489858 | tf_op jit(solution)/shard_map/concatenate | solution.py:164
  314.9 14.0 %gather_fusion.4 = bf16[1280,2048]{1,0:T(8,128)(2,1)} fusion(bf16[1281,2048]{1,0:T(8,128)(2,1)} %concatenate.23, s32[2048]{0:T(1024)S(1)} %pad_clamp_fusion), kind=kCustom, calls=%fused_computation.4 | custom fusion | bytes 10490880 | tf_op jit(solution)/shard_map/gather | solution.py:164
  328.9 4.6 all-to-all-start.4
  333.5 116.7 %all-to-all-done.4 = bf16[16,80,2048]{2,1,0:T(8,128)(2,1)} async-done(((bf16[16,80,2048]{2,1,0:T(8,128)(2,1)}), bf16[16,80,2048]{2,1,0:T(8,128)(2,1)}, u32[]{:S(2)}, u32[]{:S(2)}) %all-to-all-start.4) | async-done | bytes 5242912 | tf_op jit(solution)/shard_map/all_to_all | solution.py:167
  450.3 12.2 %gather_fusion.5 = bf16[1024,2048]{1,0:T(8,128)(2,1)} fusion(bf16[1280,2048]{1,0:T(8,128)(2,1)} %bitcast.33, s32[1024]{0:T(1024)S(1)} %broadcast_clamp_fusion), kind=kCustom, calls=%fused_computation.5 | custom fusion | bytes 8392704 | tf_op jit(solution)/shard_map/gather | solution.py:170
  462.5 5.1 %convert_reduce_fusion = f32[128,2048]{1,0:T(8,128)S(1)} fusion(bf16[1024,2048]{1,0:T(8,128)(2,1)} %gather_fusion.5), kind=kLoop, calls=%fused_computation.9 | loop fusion | flops 3932160 | bytes 5242880 | tf_op jit(solution)/shard_map/reduce_sum | solution.py:171
  (93 shorter events, 31.4 us)
Async XLA Ops:
  6.5 285.7 %copy-start = (bf16[1,768,2048]{2,1,0:T(8,128)(2,1)S(1)}, bf16[1,768,2048]{2,1,0:T(8,128)(2,1)}, u32[]{:S(2)}) copy-start(bf16[1,768,2048]{2,1,0:T(8,128)(2,1)} %param.23) | copy-start | bytes 9437188
  6.5 24.6 %copy-start.10 = (bf16[1,128,8]{1,2,0:T(8,128)(2,1)S(1)}, bf16[1,128,8]{1,2,0:T(8,128)(2,1)}, u32[]{:S(2)}) copy-start(bf16[1,128,8]{1,2,0:T(8,128)(2,1)} %param.20) | copy-start | bytes 6148
  6.5 24.9 %copy-start.8 = (s32[1,128,8]{1,2,0:T(8,128)S(1)}, s32[1,128,8]{1,2,0:T(8,128)}, u32[]{:S(2)}) copy-start(s32[1,128,8]{1,2,0:T(8,128)} %param.19) | copy-start | bytes 12292
  6.5 25.6 %copy-start.6 = (bf16[1,128,256]{2,1,0:T(8,128)(2,1)S(1)}, bf16[1,128,256]{2,1,0:T(8,128)(2,1)}, u32[]{:S(2)}) copy-start(bf16[1,128,256]{2,1,0:T(8,128)(2,1)} %param.14) | copy-start | bytes 196612
  6.5 44.3 %copy-start.7 = (bf16[1,128,256]{2,1,0:T(8,128)(2,1)S(1)}, bf16[1,128,256]{2,1,0:T(8,128)(2,1)}, u32[]{:S(2)}) copy-start(bf16[1,128,256]{2,1,0:T(8,128)(2,1)} %param.15) | copy-start | bytes 196612
  6.5 112.0 %all-gather.2.cloned.1.call-start = ((), (), s32[]{:S(2)}) async-start(), calls=%async_computation.5 | async-start | bytes 10485760 | tf_op jit(solution)/shard_map/all_gather | solution.py:98
  26.9 32.0 %all-to-all-start = ((bf16[4,2,32768]{2,1,0:T(2,128)(2,1)}), bf16[4,2,32768]{2,1,0:T(2,128)(2,1)}, u32[]{:S(2)}, u32[]{:S(2)}) async-start(bf16[4,2,32768]{2,1,0:T(2,128)(2,1)} %reshape.276), calls=%async_computation | async-start | bytes 1048576 | tf_op jit(solution)/shard_map/all_to_all | solution.py:74
  66.6 4.5 copy-start.5
  73.5 16.8 %copy-start.9 = (bf16[2048]{0:T(1024)(128)(2,1)S(1)}, bf16[2048]{0:T(1024)(128)(2,1)}, u32[]{:S(2)}) copy-start(bf16[2048]{0:T(1024)(128)(2,1)} %param.18) | copy-start | bytes 12292
  86.1 17.2 %all-to-all-start.1 = ((bf16[4,2,32768]{2,1,0:T(2,128)(2,1)}), bf16[4,2,32768]{2,1,0:T(2,128)(2,1)}, u32[]{:S(2)}, u32[]{:S(2)}) async-start(bf16[4,2,32768]{2,1,0:T(2,128)(2,1)} %reshape.278), calls=%async_computation.1 | async-start | bytes 1048576 | tf_op jit(solution)/shard_map/all_to_all | solution.py:95
  103.4 34.2 %all-to-all-start.2 = ((bf16[16,1,80]{2,1,0:T(2,128)(2,1)}), bf16[16,1,80]{2,1,0:T(2,128)(2,1)S(1)}, u32[]{:S(2)}, u32[]{:S(2)}) async-start(bf16[16,1,80]{2,1,0:T(2,128)(2,1)} %all_to_all.47), calls=%async_computation.2 | async-start | bytes 16384 | tf_op jit(solution)/shard_map/all_to_all | solution.py:128
  123.5 1.0 copy-start.2
  137.5 122.9 %all-to-all-start.3 = ((bf16[16,80,2048]{2,1,0:T(8,128)(2,1)}), bf16[16,80,2048]{2,1,0:T(8,128)(2,1)}, u32[]{:S(2)}, u32[]{:S(2)}) async-start(bf16[16,80,2048]{2,1,0:T(8,128)(2,1)} %bitcast.122), calls=%async_computation.3 | async-start | bytes 10485760 | tf_op jit(solution)/shard_map/all_to_all | solution.py:127
  280.1 7.3 %copy-start.4 = (bf16[1280,2048]{1,0:T(8,128)(2,1)S(1)}, bf16[1280,2048]{1,0:T(8,128)(2,1)}, u32[]{:S(2)}) copy-start(bf16[1280,2048]{1,0:T(8,128)(2,1)} %gather_fusion.3) | copy-start | bytes 15728644
  280.1 7.3 %copy-start.11 = (bf16[1,2048,768]{2,1,0:T(8,128)(2,1)S(1)}, bf16[1,2048,768]{2,1,0:T(8,128)(2,1)}, u32[]{:S(2)}) copy-start(bf16[1,2048,768]{2,1,0:T(8,128)(2,1)} %param.22) | copy-start | bytes 9437188
  328.9 121.3 %all-to-all-start.4 = ((bf16[16,80,2048]{2,1,0:T(8,128)(2,1)}), bf16[16,80,2048]{2,1,0:T(8,128)(2,1)}, u32[]{:S(2)}, u32[]{:S(2)}) async-start(bf16[16,80,2048]{2,1,0:T(8,128)(2,1)} %bitcast.123), calls=%async_computation.4 | async-start | bytes 10485760 | tf_op jit(solution)/shard_map/all_to_all | solution.py:167
  450.3 18.3 %copy-start.1 = (bf16[1,768,2048]{2,1,0:T(8,128)(2,1)S(1)}, bf16[1,768,2048]{2,1,0:T(8,128)(2,1)}, u32[]{:S(2)}) copy-start(bf16[1,768,2048]{2,1,0:T(8,128)(2,1)} %param.23) | copy-start | bytes 9437188
  462.5 5.1 %copy-start.3 = (f32[128,2048]{1,0:T(8,128)S(1)}, f32[128,2048]{1,0:T(8,128)}, u32[]{:S(2)}) copy-start(f32[128,2048]{1,0:T(8,128)} %copy-done.2) | copy-start | bytes 3145732
Sparse Core Ops, SparseCore 0:
  8.9 69.4 all-gather.1
where the time goes:
time: 482 us; the launch traced here: 476 us
  waiting for transfers between devices  218 us (45%)
  local copies, waits for them, and re-layouts  123 us (26%)
  other arithmetic  35.1 us (7%)
  matrix products  30.5 us (6%)
  blocking collectives  26.7 us (6%)
  starting transfers between devices  26.6 us (6%)
  between operations  14.7 us (3%)
    all_to_all x1, waiting for transfers between devices, per_device(): lax.all_to_all(returned, ('seq', 'sub'), split_axis=0, concat_axis=0, til...  117 us
    all_to_all x1, waiting for transfers between devices, per_device(): lax.all_to_all(send_rows, ('seq', 'sub'), split_axis=0, concat_axis=0, ti...  101 us
    unnamed x34, local copies, waits for them, and re-layouts  21.1 us
    unnamed x2, other arithmetic  18.9 us
    all_gather x1, blocking collectives, per_device(): lax.all_gather(key_rows, 'seq', axis=1, tiled=True)  18.7 us
    gather x1, local copies, waits for them, and re-layouts, per_device(): jnp.concatenate([recv_rows.reshape(slots_in, D), jnp.zeros((1, D), jnp.bf...  14 us
    gather x1, local copies, waits for them, and re-layouts, per_device(): jnp.concatenate([results, jnp.zeros((1, D), jnp.bfloat16)], axis=0)[dest]  14 us
    gather x1, local copies, waits for them, and re-layouts, per_device(): gathered = back[slot_of].reshape(tokens, topk, D).astype(jnp.float32)  12.2 us
  transfers between devices with their start and end apart: 6, of which 2 were waited for; matrix products, arithmetic and copies ran while one was open for 21% of the time, Pallas kernels for 0%

commit v1 on v0

--- a/solution.py
+++ b/solution.py
@@ -1,3 +1,4 @@
+import functools
 import jax
 import jax.numpy as jnp
 from jax import lax
@@ -7,6 +8,39 @@
 HD = 128
 QH = 16
 KVH = 2
+
+
+def hold_pieces_all(here_x, dim_i, a0):
+    b_now = here_x.shape
+    w1 = here_x.reshape(*b_now[:dim_i], a0, b_now[dim_i] // a0, *b_now[dim_i + 1 :])
+    return jnp.moveaxis(w1, dim_i, 0)
+
+
+def register_shifts_all(xs, on_dim):
+    xs = jnp.moveaxis(xs, 0, on_dim)
+    current_block = xs.shape
+    return xs.reshape(
+        *current_block[:on_dim],
+        current_block[on_dim] * current_block[on_dim + 1],
+        *current_block[on_dim + 2 :]
+    )
+
+
+def _order_loads(chunk, a_name, own_rows, in_array):
+    e_next, carry = (jax.lax.axis_size(a_name), jax.lax.axis_index(a_name))
+    res = hold_pieces_all(chunk, own_rows, e_next)
+    parts_out = res
+    for dd in tuple(range(1, e_next)):
+        heard, tile_out = ((carry + dd) % e_next, (carry - dd) % e_next)
+        clean = lax.dynamic_index_in_dim(res, heard, 0)
+        moved = jax.lax.ppermute(
+            clean, axis_name=a_name, perm=tuple(((w, (w + dd) % e_next) for w in range(e_next)))
+        )
+        parts_out = lax.dynamic_update_slice_in_dim(parts_out, moved, tile_out, axis=0)
+    return register_shifts_all(parts_out, in_array)
+
+
+name_chains = functools.partial(_order_loads, a_name=("seq", "sub"), own_rows=0, in_array=0)
 
 
 def attend_head(queries, keys_one, values_one, block):
@@ -124,7 +158,7 @@
     send_rows = padded_rows[token_of_slot].reshape(experts, cap, D)
     send_gates = padded_gates[item_of_slot].reshape(experts, cap)
     recv_rows, recv_gates = (
-        lax.all_to_all(send_rows, ("seq", "sub"), split_axis=0, concat_axis=0, tiled=True),
+        name_chains(send_rows),
         lax.all_to_all(send_gates, ("seq", "sub"), split_axis=0, concat_axis=0, tiled=True),
     )
     slots_in = experts * cap

time: 482 us -> 506 us (1.050)
  starting transfers between devices: 26.6 us -> 71.4 us
  waiting for transfers between devices: 218 us -> 188 us
  local copies, waits for them, and re-layouts: 123 us -> 140 us
  blocking collectives: 26.7 us -> 17 us
    all_to_all x1 -> x0, waiting for transfers between devices: 101 us -> none  [per_device(): lax.all_to_all(send_rows, ('seq', 'sub'), split_axis=0, concat_axis=0, ti...]
    ppermute x0 -> x15, waiting for transfers between devices: none -> 64.4 us  [_order_loads(): jax.lax.ppermute(clean, axis_name=a_name, perm=tuple(((w, (w + dd) % e_ne...]
    ppermute x0 -> x15, starting transfers between devices: none -> 45.5 us  [_order_loads(): jax.lax.ppermute(clean, axis_name=a_name, perm=tuple(((w, (w + dd) % e_ne...]
    dynamic_update_slice x0 -> x14, local copies, waits for them, and re-layouts: none -> 11.6 us  [_order_loads(): lax.dynamic_update_slice_in_dim(parts_out, moved, tile_out, axis=0)]
    all_gather x1, blocking collectives: 18.7 us -> 9.25 us  [per_device(): lax.all_gather(key_rows, 'seq', axis=1, tiled=True)]
    all_to_all x1, waiting for transfers between devices: 0.01 us -> 6.6 us  [per_device(): lax.all_to_all(head_block, 'seq', split_axis=1, concat_axis=2, tiled=True)]
    all_to_all x1, starting transfers between devices: 4.57 us -> 10.9 us  [per_device(): lax.all_to_all(returned, ('seq', 'sub'), split_axis=0, concat_axis=0, til...]
    all_to_all x1 -> x0, starting transfers between devices: 6.15 us -> none  [per_device(): lax.all_to_all(send_rows, ('seq', 'sub'), split_axis=0, concat_axis=0, ti...]
  transfers between devices with their start and end apart: 6 -> 20, of which waited for: 2 -> 11; matrix products, arithmetic and copies ran while one was open for 21% -> 19% of each run, Pallas kernels for 0% -> 0%
where the time goes in v1:
time: 506 us; the launch traced here: 498 us
  waiting for transfers between devices  188 us (37%)
  local copies, waits for them, and re-layouts  140 us (28%)
  starting transfers between devices  71.4 us (14%)
  other arithmetic  35.1 us (7%)
  matrix products  30.6 us (6%)
  blocking collectives  17 us (3%)
  between operations  15.1 us (3%)
    all_to_all x1, waiting for transfers between devices, per_device(): lax.all_to_all(returned, ('seq', 'sub'), split_axis=0, concat_axis=0, til...  117 us
    ppermute x15, waiting for transfers between devices, _order_loads(): jax.lax.ppermute(clean, axis_name=a_name, perm=tuple(((w, (w + dd) % e_ne...  64.4 us
    ppermute x15, starting transfers between devices, _order_loads(): jax.lax.ppermute(clean, axis_name=a_name, perm=tuple(((w, (w + dd) % e_ne...  45.5 us
    unnamed x36, local copies, waits for them, and re-layouts  21 us
    unnamed x2, other arithmetic  18.9 us
    gather x1, local copies, waits for them, and re-layouts, per_device(): jnp.concatenate([recv_rows.reshape(slots_in, D), jnp.zeros((1, D), jnp.bf...  14 us
    gather x1, local copies, waits for them, and re-layouts, per_device(): jnp.concatenate([results, jnp.zeros((1, D), jnp.bfloat16)], axis=0)[dest]  14 us
    gather x1, local copies, waits for them, and re-layouts, per_device(): gathered = back[slot_of].reshape(tokens, topk, D).astype(jnp.float32)  12.2 us
  transfers between devices with their start and end apart: 20, of which 11 were waited for; matrix products, arithmetic and copies ran while one was open for 19% of the time, Pallas kernels for 0%

profile of v1, /device:TPU:0, one launch (start us, length us, event | category | flops | bytes accessed | tf_op | source)
XLA Modules:
  0.0 498.0 jit_solution(7794672840865573303)
XLA Ops:
  11.5 13.3 %reduce.9 = bf16[2048,128]{1,0:T(8,128)(2,1)} reduce(bf16[2048,1,128]{2,1,0:T(2,128)(2,1)} %bitcast.129, bf16[]{:T(256)} %broadcast.223), dimensions={1}, to_apply=%bitcast.95.reduce_sub_computation | reduce | bytes 1048578
  36.9 8.0 %gather_fusion = bf16[1280]{0:T(1024)(128)(2,1)S(1)} fusion(bf16[1025]{0:T(1024)(128)(2,1)S(1)} %pad_maximum_fusion, s32[2048]{0:T(1024)S(1)} %get-tuple-element.188), kind=kCustom, calls=%fused_computation | custom fusion | bytes 10240 | tf_op jit(solution)/shard_map/gather | solution.py:159
  45.6 9.3 %all_gather.9 = bf16[1,512,256]{2,1,0:T(8,128)(2,1)} all-gather(bf16[1,128,256]{2,1,0:T(8,128)(2,1)S(1)} %copy-done.7), channel_id=1, replica_groups=mesh['grp'=2,'seq'=4,'sub'=4] {'seq'}, dimensions={1}, use_global_device_ids=true | all-gather | bytes 327680 | tf_op jit(solution)/shard_map/all_gather | solution.py:110
  54.9 7.7 %all_gather.10 = bf16[1,512,256]{2,1,0:T(8,128)(2,1)S(1)} all-gather(bf16[1,128,256]{2,1,0:T(8,128)(2,1)S(1)} %copy-done.8), channel_id=1, replica_groups=mesh['grp'=2,'seq'=4,'sub'=4] {'seq'}, dimensions={1}, use_global_device_ids=true | all-gather | bytes 327680 | tf_op jit(solution)/shard_map/all_gather | solution.py:111
  62.6 6.6 %all-to-all-start.2 = ((bf16[16,1,80]{2,1,0:T(2,128)(2,1)}), bf16[16,1,80]{2,1,0:T(2,128)(2,1)S(1)}, u32[]{:S(2)}, u32[]{:S(2)}) async-start(bf16[16,1,80]{2,1,0:T(2,128)(2,1)} %all_to_all.43), calls=%async_computation.2 | async-start | bytes 16384 | tf_op jit(solution)/shard_map/all_to_all | solution.py:162
  88.7 5.5 %reduce.10 = bf16[512,512]{1,0:T(8,128)(2,1)} reduce(bf16[512,1,512]{2,1,0:T(2,128)(2,1)} %bitcast.128, bf16[]{:T(256)} %broadcast.223), dimensions={1}, to_apply=%bitcast.97.reduce_sub_computation | reduce | bytes 1048578
  102.9 6.6 %all-to-all-done.1 = bf16[4,2,32768]{2,1,0:T(2,128)(2,1)} async-done(((bf16[4,2,32768]{2,1,0:T(2,128)(2,1)}), bf16[4,2,32768]{2,1,0:T(2,128)(2,1)}, u32[]{:S(2)}, u32[]{:S(2)}) %all-to-all-start.1) | async-done | bytes 524320 | tf_op jit(solution)/shard_map/all_to_all | solution.py:129
  117.3 4.9 multiply_reduce_fusion
  124.2 11.9 %gather_fusion.2 = bf16[1280,2048]{1,0:T(8,128)(2,1)} fusion(bf16[129,2048]{1,0:T(8,128)(2,1)} %concatenate.21, s32[2048]{0:T(1024)S(1)} %get-tuple-element.187), kind=kCustom, calls=%fused_computation.2 | custom fusion | bytes 10490880 | tf_op jit(solution)/shard_map/gather | solution.py:158
  139.5 5.2 %scatter_custom_fusion.1 = s32[1281]{0:T(1024)S(1)} fusion(s32[1280]{0:T(1024)S(1)} %fusion.55, s32[1280]{0:T(1024)S(1)} %iota.44, s32[]{:T(128)} %constant.310.clone.1), kind=kCustom, calls=%fused_computation.147 | custom fusion | bytes 5128 | tf_op jit(solution)/shard_map/scatter | solution.py:174
  144.7 5.0 %collective-permute-done = bf16[1,1,80,2048]{3,2,0,1:T(8,128)(2,1)} collective-permute-done((bf16[1,1,80,2048]{3,2,0,1:T(8,128)(2,1)S(1)}, bf16[1,1,80,2048]{3,2,0,1:T(8,128)(2,1)}, u32[]{:S(2)}, u32[]{:S(2)}) %collective-permute-start) | collective-permute-done | bytes 327712 | tf_op jit(solution)/shard_map/ppermute | solution.py:36
  154.3 8.0 %gather_fusion.1 = bf16[1280]{0:T(1024)(128)(2,1)S(1)} fusion(bf16[1281]{0:T(1024)(128)(2,1)S(1)} %pad_maximum_fusion.1, s32[2048]{0:T(1024)S(1)} %pad_clamp_fusion.2), kind=kCustom, calls=%fused_computation.1 | custom fusion | bytes 10240 | tf_op jit(solution)/shard_map/gather | solution.py:179
  173.0 5.1 %collective-permute-done.2 = bf16[1,1,80,2048]{3,2,0,1:T(8,128)(2,1)S(1)} collective-permute-done((bf16[1,1,80,2048]{3,2,0,1:T(8,128)(2,1)}, bf16[1,1,80,2048]{3,2,0,1:T(8,128)(2,1)S(1)}, u32[]{:S(2)}, u32[]{:S(2)}) %collective-permute-start.2) | collective-permute-done | bytes 327712 | tf_op jit(solution)/shard_map/ppermute | solution.py:36
  178.2 15.2 %collective-permute-start.4 = (bf16[1,1,80,2048]{3,2,0,1:T(8,128)(2,1)}, bf16[1,1,80,2048]{3,2,0,1:T(8,128)(2,1)S(1)}, u32[]{:S(2)}, u32[]{:S(2)}) collective-permute-start(bf16[1,1,80,2048]{3,2,0,1:T(8,128)(2,1)} %get-tuple-element.170), channel_id=1, source_target_pairs={{0,5},{1,6},{2,7},{3,8},{4,9},{5,10},{6,11},{7,12},{8,13},{9,14},{... | collective-permute-start | bytes 983048 | tf_op jit(solution)/shard_map/ppermute | solution.py:36
  197.7 6.3 %collective-permute-done.4 = bf16[1,1,80,2048]{3,2,0,1:T(8,128)(2,1)S(1)} collective-permute-done((bf16[1,1,80,2048]{3,2,0,1:T(8,128)(2,1)}, bf16[1,1,80,2048]{3,2,0,1:T(8,128)(2,1)S(1)}, u32[]{:S(2)}, u32[]{:S(2)}) %collective-permute-start.4) | collective-permute-done | bytes 327712 | tf_op jit(solution)/shard_map/ppermute | solution.py:36
  207.6 19.7 %collective-permute-done.5 = bf16[1,1,80,2048]{3,2,0,1:T(8,128)(2,1)S(1)} collective-permute-done((bf16[1,1,80,2048]{3,2,0,1:T(8,128)(2,1)}, bf16[1,1,80,2048]{3,2,0,1:T(8,128)(2,1)S(1)}, u32[]{:S(2)}, u32[]{:S(2)}) %collective-permute-start.5) | collective-permute-done | bytes 327712 | tf_op jit(solution)/shard_map/ppermute | solution.py:36
  229.4 5.0 %collective-permute-done.6 = bf16[1,1,80,2048]{3,2,0,1:T(8,128)(2,1)S(1)} collective-permute-done((bf16[1,1,80,2048]{3,2,0,1:T(8,128)(2,1)}, bf16[1,1,80,2048]{3,2,0,1:T(8,128)(2,1)S(1)}, u32[]{:S(2)}, u32[]{:S(2)}) %collective-permute-start.6) | collective-permute-done | bytes 327712 | tf_op jit(solution)/shard_map/ppermute | solution.py:36
  238.5 5.0 %collective-permute-done.7 = bf16[1,1,80,2048]{3,2,0,1:T(8,128)(2,1)S(1)} collective-permute-done((bf16[1,1,80,2048]{3,2,0,1:T(8,128)(2,1)}, bf16[1,1,80,2048]{3,2,0,1:T(8,128)(2,1)S(1)}, u32[]{:S(2)}, u32[]{:S(2)}) %collective-permute-start.7) | collective-permute-done | bytes 327712 | tf_op jit(solution)/shard_map/ppermute | solution.py:36
  243.5 8.5 %collective-permute-start.9 = (bf16[1,1,80,2048]{3,2,0,1:T(8,128)(2,1)}, bf16[1,1,80,2048]{3,2,0,1:T(8,128)(2,1)S(1)}, u32[]{:S(2)}, u32[]{:S(2)}) collective-permute-start(bf16[1,1,80,2048]{3,2,0,1:T(8,128)(2,1)} %get-tuple-element.165), channel_id=1, source_target_pairs={{0,10},{1,11},{2,12},{3,13},{4,14},{5,15},{6,0},{7,1},{8,2},{9,3},... | collective-permute-start | bytes 983048 | tf_op jit(solution)/shard_map/ppermute | solution.py:36
  255.1 11.6 %collective-permute-done.9 = bf16[1,1,80,2048]{3,2,0,1:T(8,128)(2,1)S(1)} collective-permute-done((bf16[1,1,80,2048]{3,2,0,1:T(8,128)(2,1)}, bf16[1,1,80,2048]{3,2,0,1:T(8,128)(2,1)S(1)}, u32[]{:S(2)}, u32[]{:S(2)}) %collective-permute-start.9) | collective-permute-done | bytes 327712 | tf_op jit(solution)/shard_map/ppermute | solution.py:36
  276.5 5.7 %concatenate.22 = bf16[1281,2048]{1,0:T(8,128)(2,1)} pad(bf16[1280,2048]{1,0:T(8,128)(2,1)} %bitcast.124, bf16[]{:T(256)} %constant.306.clone.1), padding=0_1x0_0 | pad | bytes 10489858 | tf_op jit(solution)/shard_map/concatenate | solution.py:176
  282.2 14.0 %gather_fusion.3 = bf16[1280,2048]{1,0:T(8,128)(2,1)} fusion(bf16[1281,2048]{1,0:T(8,128)(2,1)} %concatenate.22, s32[2048]{0:T(1024)S(1)} %pad_clamp_fusion.2), kind=kCustom, calls=%fused_computation.3 | custom fusion | bytes 10490880 | tf_op jit(solution)/shard_map/gather | solution.py:176
  296.2 7.2 %fusion.4 = f32[1280,768]{1,0:T(8,128)S(1)} fusion(bf16[1280,2048]{1,0:T(8,128)(2,1)} %gather_fusion.3, bf16[1,2048,768]{2,1,0:T(8,128)(2,1)} %param.21), kind=kOutput, calls=%fused_computation.15 | convolution fusion | flops 4026531840 | bytes 12320768 | tf_op jit(solution)/shard_map/while/body/dot_general | solution.py:189
  308.3 6.9 %fusion.1 = f32[1280,2048]{1,0:T(8,128)} fusion(bf16[1280,768]{1,0:T(8,128)(2,1)S(1)} %fusion, bf16[1,768,2048]{2,1,0:T(8,128)(2,1)S(1)} %copy-done), kind=kOutput, calls=%fused_computation.12 | convolution fusion | flops 4026531840 | bytes 15597568 | tf_op jit(solution)/shard_map/while/body/dot_general | solution.py:193
  318.2 7.2 %while.14 = (s32[]{:T(128)}, bf16[1280,2048]{1,0:T(8,128)(2,1)}, s32[]{:T(128)}, f32[1280]{0:T(1024)S(1)}, f32[1280,2048]{1,0:T(8,128)}, /*index=5*/s32[]{:T(128)}) while((s32[]{:T(128)}, bf16[1280,2048]{1,0:T(8,128)(2,1)}, s32[]{:T(128)}, f32[1280]{0:T(1024)S(1)}, f32[1280,2048]{1,0:T(8,128)}, /*index=5*/s32[]{:T(128)}) %tuple.54), condition=%wide.region_18.19_spmd, body=%wide.region_17.18_spmd.sunk | while | flops 5242882 | bytes 15733829 | solution.py:197
  318.2 7.0 %multiply_convert_fusion.3 = bf16[1280,2048]{1,0:T(8,128)(2,1)} fusion(f32[1280,2048]{1,0:T(8,128)} %get-tuple-element.235, f32[1280]{0:T(1024)S(1)} %get-tuple-element.234), kind=kLoop, calls=%fused_computation.8.clone.1 | loop fusion | flops 5242880 | bytes 15733760 | tf_op jit(solution)/shard_map/while/body/convert_element_type | solution.py:195
  325.4 5.7 %concatenate.23 = bf16[1281,2048]{1,0:T(8,128)(2,1)} pad(bf16[1280,2048]{1,0:T(8,128)(2,1)} %get-tuple-element.147, bf16[]{:T(256)} %constant.306.clone.1), padding=0_1x0_0 | pad | bytes 10489858 | tf_op jit(solution)/shard_map/concatenate | solution.py:198
  331.0 14.0 %gather_fusion.4 = bf16[1280,2048]{1,0:T(8,128)(2,1)} fusion(bf16[1281,2048]{1,0:T(8,128)(2,1)} %concatenate.23, s32[2048]{0:T(1024)S(1)} %pad_clamp_fusion), kind=kCustom, calls=%fused_computation.4 | custom fusion | bytes 10490880 | tf_op jit(solution)/shard_map/gather | solution.py:198
  345.0 10.9 %all-to-all-start.3 = ((bf16[16,80,2048]{2,1,0:T(8,128)(2,1)}), bf16[16,80,2048]{2,1,0:T(8,128)(2,1)}, u32[]{:S(2)}, u32[]{:S(2)}) async-start(bf16[16,80,2048]{2,1,0:T(8,128)(2,1)} %bitcast.125), calls=%async_computation.3 | async-start | bytes 10485760 | tf_op jit(solution)/shard_map/all_to_all | solution.py:201
  355.9 116.8 %all-to-all-done.3 = bf16[16,80,2048]{2,1,0:T(8,128)(2,1)} async-done(((bf16[16,80,2048]{2,1,0:T(8,128)(2,1)}), bf16[16,80,2048]{2,1,0:T(8,128)(2,1)}, u32[]{:S(2)}, u32[]{:S(2)}) %all-to-all-start.3) | async-done | bytes 5242912 | tf_op jit(solution)/shard_map/all_to_all | solution.py:201
  472.7 12.2 %gather_fusion.5 = bf16[1024,2048]{1,0:T(8,128)(2,1)} fusion(bf16[1280,2048]{1,0:T(8,128)(2,1)} %bitcast.33, s32[1024]{0:T(1024)S(1)} %broadcast_clamp_fusion), kind=kCustom, calls=%fused_computation.5 | custom fusion | bytes 8392704 | tf_op jit(solution)/shard_map/gather | solution.py:204
  484.9 5.1 %convert_reduce_fusion = f32[128,2048]{1,0:T(8,128)S(1)} fusion(bf16[1024,2048]{1,0:T(8,128)(2,1)} %gather_fusion.5), kind=kLoop, calls=%fused_computation.9 | loop fusion | flops 3932160 | bytes 5242880 | tf_op jit(solution)/shard_map/reduce_sum | solution.py:205
  (139 shorter events, 108.8 us)
Async XLA Ops:
  6.5 301.7 %copy-start = (bf16[1,768,2048]{2,1,0:T(8,128)(2,1)S(1)}, bf16[1,768,2048]{2,1,0:T(8,128)(2,1)}, u32[]{:S(2)}) copy-start(bf16[1,768,2048]{2,1,0:T(8,128)(2,1)} %param.23) | copy-start | bytes 9437188
  6.5 25.0 %copy-start.10 = (bf16[2048]{0:T(1024)(128)(2,1)S(1)}, bf16[2048]{0:T(1024)(128)(2,1)}, u32[]{:S(2)}) copy-start(bf16[2048]{0:T(1024)(128)(2,1)} %param.18) | copy-start | bytes 12292
  6.5 25.0 %copy-start.11 = (bf16[1,128,8]{1,2,0:T(8,128)(2,1)S(1)}, bf16[1,128,8]{1,2,0:T(8,128)(2,1)}, u32[]{:S(2)}) copy-start(bf16[1,128,8]{1,2,0:T(8,128)(2,1)} %param.20) | copy-start | bytes 6148
  6.5 25.3 %copy-start.9 = (s32[1,128,8]{1,2,0:T(8,128)S(1)}, s32[1,128,8]{1,2,0:T(8,128)}, u32[]{:S(2)}) copy-start(s32[1,128,8]{1,2,0:T(8,128)} %param.19) | copy-start | bytes 12292
  6.5 110.7 %all-gather.2.cloned.1.call-start = ((), (), s32[]{:S(2)}) async-start(), calls=%async_computation.4 | async-start | bytes 10485760 | tf_op jit(solution)/shard_map/all_gather | solution.py:132
  7.3 38.3 %copy-start.7 = (bf16[1,128,256]{2,1,0:T(8,128)(2,1)S(1)}, bf16[1,128,256]{2,1,0:T(8,128)(2,1)}, u32[]{:S(2)}) copy-start(bf16[1,128,256]{2,1,0:T(8,128)(2,1)} %param.14) | copy-start | bytes 196612
  11.0 43.8 %copy-start.8 = (bf16[1,128,256]{2,1,0:T(8,128)(2,1)S(1)}, bf16[1,128,256]{2,1,0:T(8,128)(2,1)}, u32[]{:S(2)}) copy-start(bf16[1,128,256]{2,1,0:T(8,128)(2,1)} %param.15) | copy-start | bytes 196612
  26.9 35.7 %all-to-all-start = ((bf16[4,2,32768]{2,1,0:T(2,128)(2,1)}), bf16[4,2,32768]{2,1,0:T(2,128)(2,1)}, u32[]{:S(2)}, u32[]{:S(2)}) async-start(bf16[4,2,32768]{2,1,0:T(2,128)(2,1)} %reshape.268), calls=%async_computation | async-start | bytes 1048576 | tf_op jit(solution)/shard_map/all_to_all | solution.py:108
  62.6 33.9 %all-to-all-start.2 = ((bf16[16,1,80]{2,1,0:T(2,128)(2,1)}), bf16[16,1,80]{2,1,0:T(2,128)(2,1)S(1)}, u32[]{:S(2)}, u32[]{:S(2)}) async-start(bf16[16,1,80]{2,1,0:T(2,128)(2,1)} %all_to_all.43), calls=%async_computation.2 | async-start | bytes 16384 | tf_op jit(solution)/shard_map/all_to_all | solution.py:162
  76.9 4.5 copy-start.6
  96.5 13.0 %all-to-all-start.1 = ((bf16[4,2,32768]{2,1,0:T(2,128)(2,1)}), bf16[4,2,32768]{2,1,0:T(2,128)(2,1)}, u32[]{:S(2)}, u32[]{:S(2)}) async-start(bf16[4,2,32768]{2,1,0:T(2,128)(2,1)} %reshape.270), calls=%async_computation.1 | async-start | bytes 1048576 | tf_op jit(solution)/shard_map/all_to_all | solution.py:129
  137.2 12.5 %collective-permute-start = (bf16[1,1,80,2048]{3,2,0,1:T(8,128)(2,1)S(1)}, bf16[1,1,80,2048]{3,2,0,1:T(8,128)(2,1)}, u32[]{:S(2)}, u32[]{:S(2)}) collective-permute-start(bf16[1,1,80,2048]{3,2,0,1:T(8,128)(2,1)S(1)} %constant_dynamic-slice_fusion.14), channel_id=1, source_target_pairs={{0,1},{1,2},{2,3},{3,4},{4,5},{5,6},{6,7},{7,8},{8,9},{9,10},{10,1... | collective-permute-start | bytes 983048 | tf_op jit(solution)/shard_map/ppermute | solution.py:36
  154.2 17.1 %collective-permute-start.1 = (bf16[1,1,80,2048]{3,2,0,1:T(8,128)(2,1)}, bf16[1,1,80,2048]{3,2,0,1:T(8,128)(2,1)}, u32[]{:S(2)}, u32[]{:S(2)}) collective-permute-start(bf16[1,1,80,2048]{3,2,0,1:T(8,128)(2,1)} %get-tuple-element.173), channel_id=1, source_target_pairs={{0,2},{1,3},{2,4},{3,5},{4,6},{5,7},{6,8},{7,9},{8,10},{9,11},{10,... | collective-permute-start | bytes 983048 | tf_op jit(solution)/shard_map/ppermute | solution.py:36
  162.3 104.5 %copy-start.5 = (bf16[1,1,80,2048]{3,2,0,1:T(8,128)(2,1)S(1)}, bf16[1,1,80,2048]{3,2,0,1:T(8,128)(2,1)}, u32[]{:S(2)}) copy-start(bf16[1,1,80,2048]{3,2,0,1:T(8,128)(2,1)} %get-tuple-element.163) | copy-start | bytes 983044
  162.3 15.8 %collective-permute-start.2 = (bf16[1,1,80,2048]{3,2,0,1:T(8,128)(2,1)}, bf16[1,1,80,2048]{3,2,0,1:T(8,128)(2,1)S(1)}, u32[]{:S(2)}, u32[]{:S(2)}) collective-permute-start(bf16[1,1,80,2048]{3,2,0,1:T(8,128)(2,1)} %get-tuple-element.172), channel_id=1, source_target_pairs={{0,3},{1,4},{2,5},{3,6},{4,7},{5,8},{6,9},{7,10},{8,11},{9,12},{10... | collective-permute-start | bytes 983048 | tf_op jit(solution)/shard_map/ppermute | solution.py:36
  163.2 112.6 %collective-permute-start.14 = (bf16[1,1,80,2048]{3,2,0,1:T(8,128)(2,1)S(1)}, bf16[1,1,80,2048]{3,2,0,1:T(8,128)(2,1)S(1)}, u32[]{:S(2)}, u32[]{:S(2)}) collective-permute-start(bf16[1,1,80,2048]{3,2,0,1:T(8,128)(2,1)S(1)} %get-tuple-element.160), channel_id=1, source_target_pairs={{0,15},{1,0},{2,1},{3,2},{4,3},{5,4},{6,5},{7,6},{8,7},{9,8},{10,9... | collective-permute-start | bytes 983048 | tf_op jit(solution)/shard_map/ppermute | solution.py:36
  166.6 108.5 %collective-permute-start.13 = (bf16[1,1,80,2048]{3,2,0,1:T(8,128)(2,1)}, bf16[1,1,80,2048]{3,2,0,1:T(8,128)(2,1)S(1)}, u32[]{:S(2)}, u32[]{:S(2)}) collective-permute-start(bf16[1,1,80,2048]{3,2,0,1:T(8,128)(2,1)} %get-tuple-element.161), channel_id=1, source_target_pairs={{0,14},{1,15},{2,0},{3,1},{4,2},{5,3},{6,4},{7,5},{8,6},{9,7},{10,... | collective-permute-start | bytes 983048 | tf_op jit(solution)/shard_map/ppermute | solution.py:36
  166.6 107.7 %collective-permute-start.12 = (bf16[1,1,80,2048]{3,2,0,1:T(8,128)(2,1)}, bf16[1,1,80,2048]{3,2,0,1:T(8,128)(2,1)S(1)}, u32[]{:S(2)}, u32[]{:S(2)}) collective-permute-start(bf16[1,1,80,2048]{3,2,0,1:T(8,128)(2,1)} %get-tuple-element.162), channel_id=1, source_target_pairs={{0,13},{1,14},{2,15},{3,0},{4,1},{5,2},{6,3},{7,4},{8,5},{9,6},{10... | collective-permute-start | bytes 983048 | tf_op jit(solution)/shard_map/ppermute | solution.py:36
  171.3 22.8 %collective-permute-start.3 = (bf16[1,1,80,2048]{3,2,0,1:T(8,128)(2,1)}, bf16[1,1,80,2048]{3,2,0,1:T(8,128)(2,1)S(1)}, u32[]{:S(2)}, u32[]{:S(2)}) collective-permute-start(bf16[1,1,80,2048]{3,2,0,1:T(8,128)(2,1)} %get-tuple-element.171), channel_id=1, source_target_pairs={{0,4},{1,5},{2,6},{3,7},{4,8},{5,9},{6,10},{7,11},{8,12},{9,13},{1... | collective-permute-start | bytes 983048 | tf_op jit(solution)/shard_map/ppermute | solution.py:36
  178.2 25.9 %collective-permute-start.4 = (bf16[1,1,80,2048]{3,2,0,1:T(8,128)(2,1)}, bf16[1,1,80,2048]{3,2,0,1:T(8,128)(2,1)S(1)}, u32[]{:S(2)}, u32[]{:S(2)}) collective-permute-start(bf16[1,1,80,2048]{3,2,0,1:T(8,128)(2,1)} %get-tuple-element.170), channel_id=1, source_target_pairs={{0,5},{1,6},{2,7},{3,8},{4,9},{5,10},{6,11},{7,12},{8,13},{9,14},{... | collective-permute-start | bytes 983048 | tf_op jit(solution)/shard_map/ppermute | solution.py:36
  194.1 33.2 %collective-permute-start.5 = (bf16[1,1,80,2048]{3,2,0,1:T(8,128)(2,1)}, bf16[1,1,80,2048]{3,2,0,1:T(8,128)(2,1)S(1)}, u32[]{:S(2)}, u32[]{:S(2)}) collective-permute-start(bf16[1,1,80,2048]{3,2,0,1:T(8,128)(2,1)} %get-tuple-element.169), channel_id=1, source_target_pairs={{0,6},{1,7},{2,8},{3,9},{4,10},{5,11},{6,12},{7,13},{8,14},{9,15},... | collective-permute-start | bytes 983048 | tf_op jit(solution)/shard_map/ppermute | solution.py:36
  204.0 30.4 %collective-permute-start.6 = (bf16[1,1,80,2048]{3,2,0,1:T(8,128)(2,1)}, bf16[1,1,80,2048]{3,2,0,1:T(8,128)(2,1)S(1)}, u32[]{:S(2)}, u32[]{:S(2)}) collective-permute-start(bf16[1,1,80,2048]{3,2,0,1:T(8,128)(2,1)} %get-tuple-element.168), channel_id=1, source_target_pairs={{0,7},{1,8},{2,9},{3,10},{4,11},{5,12},{6,13},{7,14},{8,15},{9,0},... | collective-permute-start | bytes 983048 | tf_op jit(solution)/shard_map/ppermute | solution.py:36
  227.3 16.2 %collective-permute-start.7 = (bf16[1,1,80,2048]{3,2,0,1:T(8,128)(2,1)}, bf16[1,1,80,2048]{3,2,0,1:T(8,128)(2,1)S(1)}, u32[]{:S(2)}, u32[]{:S(2)}) collective-permute-start(bf16[1,1,80,2048]{3,2,0,1:T(8,128)(2,1)} %get-tuple-element.167), channel_id=1, source_target_pairs={{0,8},{1,9},{2,10},{3,11},{4,12},{5,13},{6,14},{7,15},{8,0},{9,1},... | collective-permute-start | bytes 983048 | tf_op jit(solution)/shard_map/ppermute | solution.py:36
  234.4 18.3 %collective-permute-start.8 = (bf16[1,1,80,2048]{3,2,0,1:T(8,128)(2,1)}, bf16[1,1,80,2048]{3,2,0,1:T(8,128)(2,1)S(1)}, u32[]{:S(2)}, u32[]{:S(2)}) collective-permute-start(bf16[1,1,80,2048]{3,2,0,1:T(8,128)(2,1)} %get-tuple-element.166), channel_id=1, source_target_pairs={{0,9},{1,10},{2,11},{3,12},{4,13},{5,14},{6,15},{7,0},{8,1},{9,2},... | collective-permute-start | bytes 983048 | tf_op jit(solution)/shard_map/ppermute | solution.py:36
  243.5 23.3 %collective-permute-start.9 = (bf16[1,1,80,2048]{3,2,0,1:T(8,128)(2,1)}, bf16[1,1,80,2048]{3,2,0,1:T(8,128)(2,1)S(1)}, u32[]{:S(2)}, u32[]{:S(2)}) collective-permute-start(bf16[1,1,80,2048]{3,2,0,1:T(8,128)(2,1)} %get-tuple-element.165), channel_id=1, source_target_pairs={{0,10},{1,11},{2,12},{3,13},{4,14},{5,15},{6,0},{7,1},{8,2},{9,3},... | collective-permute-start | bytes 983048 | tf_op jit(solution)/shard_map/ppermute | solution.py:36
  252.8 16.9 %collective-permute-start.10 = (bf16[1,1,80,2048]{3,2,0,1:T(8,128)(2,1)}, bf16[1,1,80,2048]{3,2,0,1:T(8,128)(2,1)S(1)}, u32[]{:S(2)}, u32[]{:S(2)}) collective-permute-start(bf16[1,1,80,2048]{3,2,0,1:T(8,128)(2,1)} %get-tuple-element.164), channel_id=1, source_target_pairs={{0,11},{1,12},{2,13},{3,14},{4,15},{5,0},{6,1},{7,2},{8,3},{9,4},{... | collective-permute-start | bytes 983048 | tf_op jit(solution)/shard_map/ppermute | solution.py:36
  266.8 6.7 %collective-permute-start.11 = (bf16[1,1,80,2048]{3,2,0,1:T(8,128)(2,1)S(1)}, bf16[1,1,80,2048]{3,2,0,1:T(8,128)(2,1)S(1)}, u32[]{:S(2)}, u32[]{:S(2)}) collective-permute-start(bf16[1,1,80,2048]{3,2,0,1:T(8,128)(2,1)S(1)} %copy-done.5), channel_id=1, source_target_pairs={{0,12},{1,13},{2,14},{3,15},{4,0},{5,1},{6,2},{7,3},{8,4},{9,5},{1... | collective-permute-start | bytes 983048 | tf_op jit(solution)/shard_map/ppermute | solution.py:36
  296.2 7.3 %copy-start.4 = (bf16[1280,2048]{1,0:T(8,128)(2,1)S(1)}, bf16[1280,2048]{1,0:T(8,128)(2,1)}, u32[]{:S(2)}) copy-start(bf16[1280,2048]{1,0:T(8,128)(2,1)} %gather_fusion.3) | copy-start | bytes 15728644
  296.2 7.3 %copy-start.12 = (bf16[1,2048,768]{2,1,0:T(8,128)(2,1)S(1)}, bf16[1,2048,768]{2,1,0:T(8,128)(2,1)}, u32[]{:S(2)}) copy-start(bf16[1,2048,768]{2,1,0:T(8,128)(2,1)} %param.22) | copy-start | bytes 9437188
  345.0 127.6 %all-to-all-start.3 = ((bf16[16,80,2048]{2,1,0:T(8,128)(2,1)}), bf16[16,80,2048]{2,1,0:T(8,128)(2,1)}, u32[]{:S(2)}, u32[]{:S(2)}) async-start(bf16[16,80,2048]{2,1,0:T(8,128)(2,1)} %bitcast.125), calls=%async_computation.3 | async-start | bytes 10485760 | tf_op jit(solution)/shard_map/all_to_all | solution.py:201
  472.7 18.3 %copy-start.1 = (bf16[1,768,2048]{2,1,0:T(8,128)(2,1)S(1)}, bf16[1,768,2048]{2,1,0:T(8,128)(2,1)}, u32[]{:S(2)}) copy-start(bf16[1,768,2048]{2,1,0:T(8,128)(2,1)} %param.23) | copy-start | bytes 9437188
  484.9 5.1 %copy-start.3 = (f32[128,2048]{1,0:T(8,128)S(1)}, f32[128,2048]{1,0:T(8,128)}, u32[]{:S(2)}) copy-start(f32[128,2048]{1,0:T(8,128)} %copy-done.2) | copy-start | bytes 3145732
  (1 other events, 1.0 us)
Sparse Core Ops, SparseCore 0:
  8.9 69.4 all-gather.1
